TPU v7x, 128 devices: a whole 4x4x4 slice. The times are simulated.
128 devices in a mesh: layer: 16 (over z_lo, x, core), lat: 8 (over z_hi, y).
Axes of the slice: x: 4, y: 4, z: 4 (z_hi: 2, z_lo: 2; z = z_hi * 2 + z_lo), core: 2. Of those that a mesh axis runs over, the one named last changes fastest.
Arguments:
- saved_codes: bfloat16 [16, 512, 1024], P('layer', 'lat'), may hold values from 0.049804688 to 2
- relu_mask: int32 [16, 512, 1024], P('layer', 'lat'), may hold values 0 or 1
- errors: bfloat16 [16, 1024, 4096], P('layer'), may hold values from -0.29882812 to 0.29882812
- decoders: bfloat16 [16, 16, 512, 4096], P('layer', None, 'lat'), may hold values from -0.59765625 to 0.59765625
- inputs: bfloat16 [16, 1024, 4096], P('layer'), may hold values from -0.3984375 to 0.3984375
Outputs:
- decoder_grad: bfloat16 [16, 16, 512, 4096], P('layer', None, 'lat')
- code_grad: float32 [16, 512, 1024], P('layer', 'lat')
- encoder_grad: bfloat16 [16, 512, 4096], P('layer', 'lat')
All inputs are finite; a program needn't handle non-finite values. No bound on the sum of `relu_mask` on one device may be relied on, other than what follows from the above.
Results may differ from a plain program's by a relative error of at most 0.0049.
Values may be sent and summed in bfloat16 or wider, within the bound.
No kernel may reach another device: no remote copies, remote signals or barrier semaphores. Data moves between devices by JAX's collectives and lax.ppermute only.
A program may use at most 128 MiB of HBM per device.

v0:
```python
import jax
import jax.numpy as jnp
from jax import lax
from jax.sharding import PartitionSpec as P


def body(saved_codes, relu_mask, errors, decoders, inputs):
    target = lax.axis_index("layer")
    target_error = errors[0]
    latents = saved_codes.shape[1]
    tokens = saved_codes.shape[2]
    model_width = target_error.shape[1]
    active = saved_codes * relu_mask.astype(jnp.bfloat16)
    gathered = lax.all_gather(active, "layer", axis=0, tiled=True)
    row_count = gathered.shape[0]
    allowed = (jnp.arange(row_count, dtype=jnp.int32) <= target)[:, None, None]

    def decoder_compute():
        products = jnp.dot(
            gathered.reshape(row_count * latents, tokens),
            target_error,
            preferred_element_type=jnp.float32,
        )
        products = products.reshape(row_count, latents, model_width)
        return jnp.where(allowed, products, 0.0).astype(jnp.bfloat16)

    def decoder_skipped():
        return jnp.zeros((row_count, latents, model_width), jnp.bfloat16)

    decoder_grad = lax.cond(jnp.int32(0) <= target, decoder_compute, decoder_skipped)
    code_row_count = 1 * lax.axis_size("layer")
    code_allowed = (jnp.arange(code_row_count, dtype=jnp.int32) <= target)[:, None, None]

    def code_compute():
        slab_rows = decoders[0]
        products = lax.dot_general(
            slab_rows.reshape(code_row_count * latents, model_width),
            target_error,
            (((1,), (1,)), ((), ())),
            preferred_element_type=jnp.float32,
        )
        products = products.reshape(code_row_count, latents, tokens)
        return jnp.where(code_allowed, products, 0.0)

    def code_skipped():
        return jnp.zeros((code_row_count, latents, tokens), jnp.float32)

    code_grad = lax.psum_scatter(
        lax.cond(jnp.int32(0) <= target, code_compute, code_skipped),
        "layer",
        scatter_dimension=0,
        tiled=True,
    )
    pre_grad = (code_grad[0] * relu_mask[0].astype(jnp.float32)).astype(jnp.bfloat16)
    encoder_grad = jnp.dot(pre_grad, inputs[0], preferred_element_type=jnp.float32).astype(
        jnp.bfloat16
    )
    return (decoder_grad[None], code_grad, encoder_grad[None])


def solution(mesh):
    return jax.shard_map(
        body,
        mesh=mesh,
        in_specs=(
            P("layer", "lat", None),
            P("layer", "lat", None),
            P("layer", None, None),
            P("layer", None, "lat", None),
            P("layer", None, None),
        ),
        out_specs=(P("layer", None, "lat", None), P("layer", "lat", None), P("layer", "lat", None)),
        check_vma=False,
    )
```

profile of v0, /device:TPU:0, one launch (start us, length us, event | category | flops | bytes accessed | tf_op | source)
XLA Modules:
  0.0 129.6 jit_solution(15806542635642984849)
XLA Ops:
  7.2 0.0 all-gather.2.cloned.1.call-start
  7.2 1.7 %convert_multiply_fusion = bf16[1,64,1024]{2,1,0:T(8,128)(2,1)} fusion(bf16[1,64,1024]{2,1,0:T(8,128)(2,1)} %param.9, s32[1,64,1024]{2,1,0:T(8,128)} %param.10), kind=kLoop, calls=%fused_computation.14 | loop fusion | flops 131072 | bytes 524288 | tf_op jit(solution)/shard_map/mul | solution.py:13
  8.9 0.0 all-gather.2.cloned.1.call-update
  8.9 0.0 reduce-scatter.2.cloned.1.call-start
  9.0 15.1 %conditional.3 = (f32[16,64,1024]{2,1,0:T(8,128)}) conditional(s32[]{:T(128)} %convert_element_type.23, () %tuple.24, (pred[16,1,1]{0,2,1:T(4,128)(4,1)S(1)}, bf16[1,16,64,4096]{3,2,1,0:T(8,128)(2,1)}, bf16[1024,4096]{1,0:T(8,128)(2,1)}) %tuple.35), branch_computations={%region_2.3_spmd, %region_3.4_spmd} | conditional | flops 8590983168 | bytes 20971544 | solution.py:49
  9.0 15.1 %broadcast_select_fusion = f32[16,64,1024]{2,1,0:T(8,128)} fusion(pred[16]{0:T(512)(128)(4,1)S(1)} %bitcast.35, bf16[1024,4096]{1,0:T(8,128)(2,1)} %get-tuple-element.24, bf16[1,16,64,4096]{3,2,1,0:T(8,128)(2,1)} %get-tuple-element.29), kind=kOutput, calls=%fused_computation.7 | convolution fusion | flops 8590983168 | bytes 20971536 | tf_op jit(solution)/shard_map/cond/branch_1_fun/dot_general | solution.py:36
  24.1 0.0 reduce-scatter.2.cloned.1.call-update
  24.1 22.5 %all-gather.2.cloned.1.call-done = bf16[16,64,1024]{2,1,0:T(8,128)(2,1)} async-done(((bf16[1,64,1024]{2,1,0:T(8,128)(2,1)}), bf16[16,64,1024]{2,1,0:T(8,128)(2,1)}) %all-gather.2.cloned.1.call-update) | async-done | bytes 2097168 | tf_op jit(solution)/shard_map/all_gather | solution.py:14
  46.6 0.0 copy-start
  46.6 14.8 %conditional.2 = (bf16[1,16,64,4096]{3,2,1,0:T(8,128)(2,1)}) conditional(s32[]{:T(128)} %convert_element_type.23, () %tuple.22, (pred[16,1,1]{0,2,1:T(4,128)(4,1)S(1)}, bf16[16,64,1024]{2,1,0:T(8,128)(2,1)}, bf16[1024,4096]{1,0:T(8,128)(2,1)}) %tuple.36), branch_computations={%region_0.0_spmd, %region_1.2_spmd} | conditional | flops 8598323200 | bytes 18874392 | solution.py:30
  46.6 14.8 %fusion = bf16[1,16,64,4096]{3,2,1,0:T(8,128)(2,1)} fusion(pred[16]{0:T(512)(128)(4,1)S(1)} %bitcast.36, bf16[16,64,1024]{2,1,0:T(8,128)(2,1)} %get-tuple-element.20, bf16[1024,4096]{1,0:T(8,128)(2,1)} %get-tuple-element.21), kind=kOutput, calls=%fused_computation.1 | convolution fusion | flops 8598323200 | bytes 18874384 | tf_op jit(solution)/shard_map/cond/branch_1_fun/dot_general | solution.py:19
  61.4 55.5 %reduce-scatter.2.cloned.1.call-done = f32[1,64,1024]{2,1,0:T(8,128)} async-done(((f32[16,64,1024]{2,1,0:T(8,128)}), f32[1,64,1024]{2,1,0:T(8,128)}) %reduce-scatter.2.cloned.1.call-update) | async-done | bytes 262160 | tf_op jit(solution)/shard_map/reduce_scatter | solution.py:48
  117.0 0.0 copy-done
  117.0 5.8 %fusion.17 = bf16[1,64,4096]{2,1,0:T(8,128)(2,1)} fusion(bf16[1,1024,4096]{2,1,0:T(8,128)(2,1)} %param.13, f32[1,64,1024]{2,1,0:T(8,128)} %reduce-scatter.2.cloned.1.call-done, s32[1,64,1024]{2,1,0:T(8,128)S(1)} %copy-done), kind=kOutput, calls=%fused_computation.11 | convolution fusion | flops 537329664 | bytes 9437184 | tf_op jit(solution)/shard_map/dot_general | solution.py:55
  (1 shorter events, 0.0 us)
Async XLA Ops:
  7.2 39.5 %all-gather.2.cloned.1.call-start = ((), (), s32[]{:S(2)}) async-start(), calls=%async_computation.1 | async-start | bytes 2228224 | tf_op jit(solution)/shard_map/all_gather | solution.py:14
  8.9 108.0 %reduce-scatter.2.cloned.1.call-start = ((), (), s32[]{:S(2)}) async-start(), calls=%async_computation.2 | async-start | bytes 4456448 | tf_op jit(solution)/shard_map/reduce_scatter | solution.py:48
  46.6 70.3 %copy-start = (s32[1,64,1024]{2,1,0:T(8,128)S(1)}, s32[1,64,1024]{2,1,0:T(8,128)}, u32[]{:S(2)}) copy-start(s32[1,64,1024]{2,1,0:T(8,128)} %param.10) | copy-start | bytes 786436
Sparse Core Ops, SparseCore 0:
  10.2 36.3 all-gather.1
  49.6 67.3 reduce-scatter.1
where the time goes:
time: 130 us
  waiting for transfers between devices  78.1 us (60%)
  matrix products  35.7 us (27%)
  between operations  14 us (11%)
  other arithmetic  1.71 us (1%)
    reduce_scatter x1, waiting for transfers between devices, body(): lax.psum_scatter(lax.cond(jnp.int32(0) <= target, code_compute, code_skip...  55.5 us
    all_gather x1, waiting for transfers between devices, body(): gathered = lax.all_gather(active, 'layer', axis=0, tiled=True)  22.5 us
    dot_general x1, matrix products, code_compute(): lax.dot_general(slab_rows.reshape(code_row_count * latents, model_width),...  15.1 us
    dot_general x1, matrix products, decoder_compute(): jnp.dot(gathered.reshape(row_count * latents, tokens), target_error, pref...  14.8 us
    dot_general x1, matrix products, body(): jnp.dot(pre_grad, inputs[0], preferred_element_type=jnp.float32)  5.84 us
  transfers between devices with their start and end apart: 2, of which 2 were waited for; matrix products, arithmetic and copies ran while one was open for 23% of the time, Pallas kernels for 0%

commit v1 on v0

--- a/solution.py
+++ b/solution.py
@@ -11,7 +11,8 @@
     tokens = saved_codes.shape[2]
     model_width = target_error.shape[1]
     active = saved_codes * relu_mask.astype(jnp.bfloat16)
-    gathered = lax.all_gather(active, "layer", axis=0, tiled=True)
+    outgoing = jnp.stack([active] * lax.axis_size("layer"))
+    gathered = jnp.concatenate(lax.all_to_all(outgoing, "layer", 0, 0), axis=0)
     row_count = gathered.shape[0]
     allowed = (jnp.arange(row_count, dtype=jnp.int32) <= target)[:, None, None]
 

time: 130 us -> 119 us (0.915)
  waiting for transfers between devices: 78.1 us -> 61.5 us
  starting transfers between devices: 0.08 us -> 5.91 us
  other arithmetic: 1.71 us -> 0.03 us
  local copies, waits for them, and re-layouts: 0.01 us -> 1.59 us
    all_to_all x0 -> x1, waiting for transfers between devices: none -> 33.6 us  [body(): gathered = jnp.concatenate(lax.all_to_all(outgoing, 'layer', 0, 0), axis=0)]
    reduce_scatter x1, waiting for transfers between devices: 55.5 us -> 27.9 us  [body(): lax.psum_scatter(lax.cond(jnp.int32(0) <= target, code_compute, code_skip...]
    all_gather x1 -> x0, waiting for transfers between devices: 22.5 us -> none  [body(): gathered = lax.all_gather(active, 'layer', axis=0, tiled=True)]
    all_to_all x0 -> x1, starting transfers between devices: none -> 5.87 us  [body(): gathered = jnp.concatenate(lax.all_to_all(outgoing, 'layer', 0, 0), axis=0)]
    mul x1, other arithmetic: 1.7 us -> 0.02 us  [body(): active = saved_codes * relu_mask.astype(jnp.bfloat16)]
    another operation x0 -> x1, local copies, waits for them, and re-layouts: none -> 1.58 us  [body(): outgoing = jnp.stack([active] * lax.axis_size('layer'))]
  transfers between devices with their start and end apart: 2 -> 2, of which waited for: 2 -> 2; matrix products, arithmetic and copies ran while one was open for 23% -> 14% of each run, Pallas kernels for 0% -> 0%
where the time goes in v1:
time: 119 us
  waiting for transfers between devices  61.5 us (52%)
  matrix products  35.4 us (30%)
  between operations  14.1 us (12%)
  starting transfers between devices  5.91 us (5%)
  local copies, waits for them, and re-layouts  1.59 us (1%)
    all_to_all x1, waiting for transfers between devices, body(): gathered = jnp.concatenate(lax.all_to_all(outgoing, 'layer', 0, 0), axis=0)  33.6 us
    reduce_scatter x1, waiting for transfers between devices, body(): lax.psum_scatter(lax.cond(jnp.int32(0) <= target, code_compute, code_skip...  27.9 us
    dot_general x1, matrix products, code_compute(): lax.dot_general(slab_rows.reshape(code_row_count * latents, model_width),...  15.1 us
    dot_general x1, matrix products, decoder_compute(): jnp.dot(gathered.reshape(row_count * latents, tokens), target_error, pref...  14.5 us
    all_to_all x1, starting transfers between devices, body(): gathered = jnp.concatenate(lax.all_to_all(outgoing, 'layer', 0, 0), axis=0)  5.87 us
    dot_general x1, matrix products, body(): jnp.dot(pre_grad, inputs[0], preferred_element_type=jnp.float32)  5.84 us
  transfers between devices with their start and end apart: 2, of which 2 were waited for; matrix products, arithmetic and copies ran while one was open for 14% of the time, Pallas kernels for 0%

profile of v1, /device:TPU:0, one launch (start us, length us, event | category | flops | bytes accessed | tf_op | source)
XLA Modules:
  0.0 118.6 jit_solution(13911508905482915515)
XLA Ops:
  7.2 0.0 reduce-scatter.2.cloned.1.call-start
  7.2 0.0 copy-start
  7.2 0.0 copy-start.1
  7.2 15.1 %conditional.3 = (f32[16,64,1024]{2,1,0:T(8,128)}) conditional(s32[]{:T(128)} %convert_element_type.23, () %tuple.24, (pred[16,1,1]{0,2,1:T(4,128)(4,1)S(1)}, bf16[1,16,64,4096]{3,2,1,0:T(8,128)(2,1)}, bf16[1024,4096]{1,0:T(8,128)(2,1)}) %tuple.34), branch_computations={%region_2.3_spmd, %region_3.4_spmd} | conditional | flops 8590983168 | bytes 20971544 | solution.py:50
  7.3 15.1 %broadcast_select_fusion = f32[16,64,1024]{2,1,0:T(8,128)} fusion(pred[16]{0:T(512)(128)(4,1)S(1)} %bitcast.40, bf16[1024,4096]{1,0:T(8,128)(2,1)} %get-tuple-element.24, bf16[1,16,64,4096]{3,2,1,0:T(8,128)(2,1)} %get-tuple-element.29), kind=kOutput, calls=%fused_computation.8 | convolution fusion | flops 8590983168 | bytes 20971536 | tf_op jit(solution)/shard_map/cond/branch_1_fun/dot_general | solution.py:37
  22.4 0.0 reduce-scatter.2.cloned.1.call-update
  22.4 0.0 copy-done
  22.4 0.0 copy-done.1
  22.4 1.6 %stack.2 = bf16[16,1,64,1024]{3,2,1,0:T(8,128)(2,1)} broadcast(bf16[64,1024]{1,0:T(8,128)(2,1)S(1)} %multiply_bitcast_fusion), dimensions={2,3} | broadcast | bytes 2228224 | tf_op jit(solution)/shard_map/stack | solution.py:14
  24.0 5.9 %all-to-all-start = ((bf16[16,1,64,1024]{3,2,1,0:T(8,128)(2,1)}), bf16[16,1,64,1024]{3,2,1,0:T(8,128)(2,1)S(1)}, u32[]{:S(2)}, u32[]{:S(2)}) async-start(bf16[16,1,64,1024]{3,2,1,0:T(8,128)(2,1)} %stack.2), calls=%async_computation | async-start | bytes 4194304 | tf_op jit(solution)/shard_map/all_to_all | solution.py:15
  29.9 33.6 %all-to-all-done = bf16[16,1,64,1024]{3,2,1,0:T(8,128)(2,1)S(1)} async-done(((bf16[16,1,64,1024]{3,2,1,0:T(8,128)(2,1)}), bf16[16,1,64,1024]{3,2,1,0:T(8,128)(2,1)S(1)}, u32[]{:S(2)}, u32[]{:S(2)}) %all-to-all-start) | async-done | bytes 2097184 | tf_op jit(solution)/shard_map/all_to_all | solution.py:15
  63.5 14.5 %conditional.2 = (bf16[1,16,64,4096]{3,2,1,0:T(8,128)(2,1)}) conditional(s32[]{:T(128)} %convert_element_type.23, () %tuple.22, (pred[16,1,1]{0,2,1:T(4,128)(4,1)S(1)}, bf16[16,1,64,1024]{3,2,1,0:T(8,128)(2,1)S(1)}, bf16[1024,4096]{1,0:T(8,128)(2,1)}) %tuple.35), branch_computations={%region_0.0_spmd, %region_1.2_spmd} | conditional | flops 8598323200 | bytes 18874392 | solution.py:31
  63.5 14.5 %fusion = bf16[1,16,64,4096]{3,2,1,0:T(8,128)(2,1)} fusion(pred[16]{0:T(512)(128)(4,1)S(1)} %bitcast.41, bf16[1024,4096]{1,0:T(8,128)(2,1)} %get-tuple-element.21, bf16[16,1,64,1024]{3,2,1,0:T(8,128)(2,1)S(1)} %get-tuple-element.31), kind=kOutput, calls=%fused_computation.1 | convolution fusion | flops 8598323200 | bytes 18874384 | tf_op jit(solution)/shard_map/cond/branch_1_fun/dot_general | solution.py:20
  78.0 27.9 %reduce-scatter.2.cloned.1.call-done = f32[1,64,1024]{2,1,0:T(8,128)} async-done(((f32[16,64,1024]{2,1,0:T(8,128)}), f32[1,64,1024]{2,1,0:T(8,128)}) %reduce-scatter.2.cloned.1.call-update) | async-done | bytes 262160 | tf_op jit(solution)/shard_map/reduce_scatter | solution.py:49
  105.9 5.8 %fusion.18 = bf16[1,64,4096]{2,1,0:T(8,128)(2,1)} fusion(bf16[1,1024,4096]{2,1,0:T(8,128)(2,1)} %param.13, f32[1,64,1024]{2,1,0:T(8,128)} %reduce-scatter.2.cloned.1.call-done, s32[1,64,1024]{2,1,0:T(8,128)S(1)} %copy-done), kind=kOutput, calls=%fused_computation.12 | convolution fusion | flops 537329664 | bytes 9437184 | tf_op jit(solution)/shard_map/dot_general | solution.py:56
  (2 shorter events, 0.0 us)
Async XLA Ops:
  7.2 98.7 %reduce-scatter.2.cloned.1.call-start = ((), (), s32[]{:S(2)}) async-start(), calls=%async_computation.2 | async-start | bytes 4456448 | tf_op jit(solution)/shard_map/reduce_scatter | solution.py:49
  7.2 15.2 %copy-start = (s32[1,64,1024]{2,1,0:T(8,128)S(1)}, s32[1,64,1024]{2,1,0:T(8,128)}, u32[]{:S(2)}) copy-start(s32[1,64,1024]{2,1,0:T(8,128)} %param.10) | copy-start | bytes 786436
  7.2 15.2 %copy-start.1 = (bf16[1,64,1024]{2,1,0:T(8,128)(2,1)S(1)}, bf16[1,64,1024]{2,1,0:T(8,128)(2,1)}, u32[]{:S(2)}) copy-start(bf16[1,64,1024]{2,1,0:T(8,128)(2,1)} %param.9) | copy-start | bytes 393220
  24.0 39.5 %all-to-all-start = ((bf16[16,1,64,1024]{3,2,1,0:T(8,128)(2,1)}), bf16[16,1,64,1024]{3,2,1,0:T(8,128)(2,1)S(1)}, u32[]{:S(2)}, u32[]{:S(2)}) async-start(bf16[16,1,64,1024]{3,2,1,0:T(8,128)(2,1)} %stack.2), calls=%async_computation | async-start | bytes 4194304 | tf_op jit(solution)/shard_map/all_to_all | solution.py:15
Sparse Core Ops, SparseCore 0:
  22.5 83.3 reduce-scatter.1
